TPU v7x, 32 devices: a whole 2x2x4 slice. The times are simulated.
32 devices in a mesh: rep: 8 (over z, y), zero: 4 (over x, core).
Axes of the slice: x: 2, y: 2, z: 4, core: 2. Of those that a mesh axis runs over, the one named last changes fastest.
Arguments:
- tokens: bfloat16 [12288, 1280], P(('rep', 'zero')), may hold values from -6 to 6
- cotangent: bfloat16 [12288, 1280], P(('rep', 'zero')), may hold values from -6 to 6
- weights: bfloat16 [1280, 6, 1280], P('zero')
- vectors: bfloat16 [5, 1280], P(None, 'zero')
- error: float32 [10240, 6, 1280], P(('rep', 'zero'))
- previous_right_factors: float32 [6, 1280, 32], P(None, None, 'zero'), may hold values from -6 to 6
- momentum: float32 [1280, 6, 1280], P('zero', None, 'rep')
- vec_momentum: float32 [5, 1280], P(None, 'zero')
- prompt_len: int32 [8], P('rep'), may hold values from 512 to 1024, as said below
Outputs:
- result: bfloat16 [12288, 1280], P(('rep', 'zero'))
- grad_tokens: float32 [12288, 1280], P(('rep', 'zero'))
- grad_weights: float32 [1280, 6, 1280], P('zero', None, 'rep')
- grad_vectors: float32 [5, 1280], P(None, 'zero')
- new_error: float32 [10240, 6, 1280], P(('rep', 'zero'))
- fresh_right_factors: float32 [6, 1280, 32], P(None, None, 'zero')
- new_momentum: float32 [1280, 6, 1280], P('zero', None, 'rep')
- new_vec_momentum: float32 [5, 1280], P(None, 'zero')
- update_weights: float32 [1280, 6, 1280], P('zero', None, 'rep')
- update_vectors: float32 [5, 1280], P(None, 'zero')
Inputs may be any that keep to these rules, and one draw needn't show every extreme that they name: `prompt_len`: valid prompt rows of a group; the other prompt rows of its 1024 are padding.
All inputs are finite; a program needn't handle non-finite values.
Results may differ from a plain program's by a relative error of at most 0.028.
Values may be sent and summed in bfloat16 or wider, within the bound.
No kernel may reach another device: no remote copies, remote signals or barrier semaphores. Data moves between devices by JAX's collectives and lax.ppermute only.
A program may use at most 320 MiB of HBM per device.

v0:
```python
import math
import jax
import jax.numpy as jnp
from jax import lax
from jax.sharding import PartitionSpec as P

HEADS = 16
PROMPT = 1024
EPS = 1e-06
MU = 0.9
LOG2E = 1.442695041
NEG = -1e30
PRECISION_HIGH = lax.Precision.HIGHEST


def rms_scale(field):
    return lax.rsqrt(jnp.mean(field * field, axis=-1, keepdims=True) + EPS)


def norm_back(field, scale, gain_vec, grad_in):
    weighted = grad_in * gain_vec
    inner = jnp.mean(field * weighted, axis=-1, keepdims=True)
    return scale * weighted - field * (scale * scale * scale) * inner


def orthonormal(factor):
    columns = []
    for col_index in range(factor.shape[-1]):
        column = factor[..., col_index]
        for earlier in columns:
            column = column - jnp.sum(earlier * column, axis=-2, keepdims=True) * earlier
        column = column * lax.rsqrt(jnp.sum(column * column, axis=-2, keepdims=True) + EPS)
        columns.append(column)
    return jnp.stack(columns, axis=-1)


def on_device(
    tokens,
    cotangent,
    weights,
    vectors,
    error,
    previous_right_factors,
    momentum,
    vec_momentum,
    prompt_len,
):
    f32 = jnp.float32
    bf16 = jnp.bfloat16
    zero_index = lax.axis_index("zero")
    rep_index = lax.axis_index("rep")
    zero_count = lax.axis_size("zero")
    rep_count = lax.axis_size("rep")
    tok_rows, feat_width = tokens.shape
    head_dim = feat_width // HEADS
    prompt_rows = PROMPT // zero_count
    prompt_valid = prompt_len[0]
    full_w, full_v = (
        lax.all_gather(weights, "zero", axis=0, tiled=True),
        lax.all_gather(vectors, "zero", axis=1, tiled=True),
    )
    vec_float = full_v.astype(f32)
    gain_one = vec_float[0]
    gain_two = vec_float[1]
    bias_one = vec_float[2]
    bias_two = vec_float[3]
    scale_raw = vec_float[4]
    tok_float = tokens.astype(f32)
    scale_one = rms_scale(tok_float)
    normed_one = (tok_float * scale_one * gain_one).astype(bf16)
    projected = jnp.einsum("ti,omi->mto", normed_one, full_w[:, 0:3, :], preferred_element_type=f32)
    query = projected[0]
    key_low = projected[1].astype(bf16)
    value_low = projected[2].astype(bf16)
    scale_const = LOG2E / math.sqrt(head_dim)
    query_scale = scale_const * jax.nn.softplus(scale_raw)
    scaled = (query * query_scale).astype(bf16)
    key_far, value_far = (
        lax.all_gather(key_low[:prompt_rows], "zero", axis=0, tiled=True),
        lax.all_gather(value_low[:prompt_rows], "zero", axis=0, tiled=True),
    )
    key_rows = jnp.concatenate([key_far, key_low[prompt_rows:]], axis=0)
    value_rows = jnp.concatenate([value_far, value_low[prompt_rows:]], axis=0)
    key_count = key_rows.shape[0]
    q_row = lax.broadcasted_iota(jnp.int32, (tok_rows, key_count), 0)
    k_col = lax.broadcasted_iota(jnp.int32, (tok_rows, key_count), 1)
    q_prompt = q_row < prompt_rows
    q_pos = zero_index * prompt_rows + q_row
    k_prompt = k_col < PROMPT
    see_prompt = k_prompt & (k_col < prompt_valid) & (jnp.logical_not(q_prompt) | (k_col <= q_pos))
    see_cont = (
        jnp.logical_not(k_prompt)
        & jnp.logical_not(q_prompt)
        & (k_col - PROMPT <= q_row - prompt_rows)
    )
    allowed = see_prompt | see_cont
    q_heads = scaled.reshape(tok_rows, HEADS, head_dim)
    k_heads = key_rows.reshape(key_count, HEADS, head_dim)
    v_heads = value_rows.reshape(key_count, HEADS, head_dim)

    def masked_scores():
        raw_scores = jnp.einsum("thd,khd->htk", q_heads, k_heads, preferred_element_type=f32)
        return jnp.where(allowed[None], raw_scores, NEG)

    masked = masked_scores()
    row_top = jnp.max(masked, axis=-1, keepdims=True)
    log_total = row_top + jnp.log(jnp.sum(jnp.exp(masked - row_top), axis=-1, keepdims=True))
    probs = jnp.exp(masked - log_total)
    attended = (
        jnp.einsum("htk,khd->thd", probs.astype(bf16), v_heads, preferred_element_type=f32)
        .reshape(tok_rows, feat_width)
        .astype(bf16)
    )
    branch = jnp.einsum("ti,oi->to", attended, full_w[:, 3, :], preferred_element_type=f32)
    hidden = tok_float + branch
    scale_two = rms_scale(hidden)
    normed_two = (hidden * scale_two * gain_two).astype(bf16)
    upper = (
        jnp.einsum("ti,oi->to", normed_two, full_w[:, 4, :], preferred_element_type=f32) + bias_one
    )
    activ = jax.nn.silu(upper).astype(bf16)
    output = jnp.einsum("ti,oi->to", activ, full_w[:, 5, :], preferred_element_type=f32) + bias_two
    result = (hidden + output).astype(bf16)
    back_w = lax.all_gather(weights, "zero", axis=0, tiled=True)
    grad_out = cotangent.astype(f32)
    grad_f = grad_out.astype(bf16)
    grad_act = jnp.einsum("to,oi->ti", grad_f, back_w[:, 5, :], preferred_element_type=f32)
    gate_sig = jax.nn.sigmoid(upper)
    grad_up = (grad_act * gate_sig * (1.0 + upper * (1.0 - gate_sig))).astype(bf16)
    grad_n2 = jnp.einsum("to,oi->ti", grad_up, back_w[:, 4, :], preferred_element_type=f32)
    grad_gain_two = jnp.sum(grad_n2 * hidden * scale_two, axis=0)
    grad_hidden = grad_out + norm_back(hidden, scale_two, gain_two, grad_n2)
    grad_branch = grad_hidden.astype(bf16)
    grad_att = jnp.einsum(
        "to,oi->ti", grad_branch, back_w[:, 3, :], preferred_element_type=f32
    ).astype(bf16)
    grad_att_heads = grad_att.reshape(tok_rows, HEADS, head_dim)
    probs_again = jnp.exp(masked_scores() - log_total)
    grad_probs = jnp.einsum("thd,khd->htk", grad_att_heads, v_heads, preferred_element_type=f32)
    delta = jnp.sum(probs_again * grad_probs, axis=-1, keepdims=True)
    grad_scores = (probs_again * (grad_probs - delta)).astype(bf16)
    grad_values = jnp.einsum(
        "htk,thd->khd", probs_again.astype(bf16), grad_att_heads, preferred_element_type=f32
    ).reshape(key_count, feat_width)
    grad_keys = jnp.einsum(
        "htk,thd->khd", grad_scores, q_heads, preferred_element_type=f32
    ).reshape(key_count, feat_width)
    grad_sq = jnp.einsum("htk,khd->thd", grad_scores, k_heads, preferred_element_type=f32).reshape(
        tok_rows, feat_width
    )
    own_keys, own_values = (
        lax.psum_scatter(
            grad_keys[:PROMPT].astype(jnp.bfloat16), "zero", scatter_dimension=0, tiled=True
        ).astype(jnp.float32),
        lax.psum_scatter(
            grad_values[:PROMPT].astype(jnp.bfloat16), "zero", scatter_dimension=0, tiled=True
        ).astype(jnp.float32),
    )
    grad_key = jnp.concatenate([own_keys, grad_keys[PROMPT:]], axis=0).astype(bf16)
    grad_value = jnp.concatenate([own_values, grad_values[PROMPT:]], axis=0).astype(bf16)
    grad_query = (grad_sq * query_scale).astype(bf16)
    grad_scale_raw = jnp.sum(grad_sq * query, axis=0) * scale_const * jax.nn.sigmoid(scale_raw)
    grad_proj = jnp.stack([grad_query, grad_key, grad_value], axis=0)
    grad_n1 = jnp.einsum("mto,omi->ti", grad_proj, back_w[:, 0:3, :], preferred_element_type=f32)
    grad_gain_one = jnp.sum(grad_n1 * tok_float * scale_one, axis=0)
    grad_tokens = grad_hidden + norm_back(tok_float, scale_one, gain_one, grad_n1)
    grad_stack = jnp.stack([grad_query, grad_key, grad_value, grad_branch, grad_up, grad_f], axis=0)
    input_stack = jnp.stack(
        [normed_one, normed_one, normed_one, attended, normed_two, activ], axis=0
    )
    grad_block = lax.psum_scatter(
        jnp.einsum("mto,mti->omi", grad_stack, input_stack, preferred_element_type=f32).astype(
            jnp.bfloat16
        ),
        "zero",
        scatter_dimension=0,
        tiled=True,
    ).astype(jnp.float32)
    vec_terms = jnp.stack(
        [
            grad_gain_one,
            grad_gain_two,
            jnp.sum(grad_up.astype(f32), axis=0),
            jnp.sum(grad_f.astype(f32), axis=0),
            grad_scale_raw,
        ],
        axis=0,
    )
    vec_block = lax.psum_scatter(vec_terms, "zero", scatter_dimension=1, tiled=True)
    combined_result = grad_block + error
    local_left_factor = jnp.einsum(
        "edn,dnw->edw", combined_result, previous_right_factors, precision=PRECISION_HIGH
    )
    vec_total = lax.psum(vec_block, "rep")
    left_parts = []
    right_parts = []
    for mat_index in range(combined_result.shape[1]):
        left_sum = lax.psum(local_left_factor[:, mat_index], "rep")
        left_ortho = orthonormal(left_sum[:, None, :] / rep_count)[:, 0, :]
        right_term = jnp.einsum(
            "oi,or->ir", combined_result[:, mat_index], left_ortho, precision=PRECISION_HIGH
        )
        right_parts.append(lax.psum(right_term.astype(jnp.bfloat16), "rep").astype(jnp.float32))
        left_parts.append(left_ortho)
    orthogonalized = jnp.stack(left_parts, axis=1)
    right_total = jnp.stack(right_parts, axis=0)
    fresh_right_factors = right_total / rep_count
    approximation = jnp.einsum(
        "upt,pqt->upq", orthogonalized, fresh_right_factors, precision=PRECISION_HIGH
    )
    new_error = combined_result - approximation
    rep_width = feat_width // rep_count
    grad_weights = lax.dynamic_slice_in_dim(approximation, rep_index * rep_width, rep_width, 2)
    step_rate = 0.03 / math.sqrt(zero_count * tok_rows)
    new_momentum = MU * momentum + grad_weights
    update_weights = -step_rate * new_momentum
    grad_vectors = vec_total / rep_count
    new_vec_momentum = MU * vec_momentum + grad_vectors
    update_vectors = -step_rate * new_vec_momentum
    return (
        result,
        grad_tokens,
        grad_weights,
        grad_vectors,
        new_error,
        fresh_right_factors,
        new_momentum,
        new_vec_momentum,
        update_weights,
        update_vectors,
    )


def solution(mesh):
    in_specs = (
        P(("rep", "zero"), None),
        P(("rep", "zero"), None),
        P("zero", None, None),
        P(None, "zero"),
        P(("rep", "zero"), None, None),
        P(None, None, "zero"),
        P("zero", None, "rep"),
        P(None, "zero"),
        P("rep"),
    )
    out_specs = (
        P(("rep", "zero"), None),
        P(("rep", "zero"), None),
        P("zero", None, "rep"),
        P(None, "zero"),
        P(("rep", "zero"), None, None),
        P(None, None, "zero"),
        P("zero", None, "rep"),
        P(None, "zero"),
        P("zero", None, "rep"),
        P(None, "zero"),
    )
    return jax.shard_map(
        on_device, mesh=mesh, in_specs=in_specs, out_specs=out_specs, check_vma=False
    )
```

profile of v0, /device:TPU:0, one launch (start us, length us, event | category | flops | bytes accessed | tf_op | source)
XLA Modules:
  0.0 1215.3 jit_solution(3644075702543074997)
XLA Ops:
  8.0 6.2 all-gather.2
  15.9 120.7 %all-gather.7.cloned.1.call-done = bf16[1280,6,1280]{2,0,1:T(8,128)(2,1)} async-done(((bf16[320,6,1280]{2,0,1:T(8,128)(2,1)}), bf16[1280,6,1280]{2,0,1:T(8,128)(2,1)}) %all-gather.7.cloned.1.call-update) | async-done | bytes 19660816 | tf_op jit(solution)/shard_map/all_gather | solution.py:59
  136.6 10.4 fusion.115
  163.3 12.1 all-gather.9.cloned.1.call-done
  175.4 27.7 %all-gather.11.cloned.1.call-done = bf16[1,1024,1280]{2,1,0:T(8,128)(2,1)} async-done(((bf16[1,256,1280]{2,1,0:T(8,128)(2,1)}), bf16[1,1024,1280]{2,1,0:T(8,128)(2,1)}) %all-gather.11.cloned.1.call-update) | async-done | bytes 2621456 | tf_op jit(solution)/shard_map/all_gather | solution.py:79
  203.1 4.6 pad_maximum_fusion
  207.7 5.4 copy.80
  213.2 5.4 copy.82
  218.6 13.1 %select_reduce_fusion = (f32[16,384]{1,0:T(8,128)S(1)}, f32[16,384,1152]{2,1,0:T(8,128)}) fusion(pred[384,1152]{1,0:T(8,128)(4,1)} %fusion.50, bf16[1152,16,80]{0,2,1:T(8,128)(2,1)} %bitcast.662, f32[384,16,80]{0,2,1:T(8,128)S(1)} %bitcast.659, f32[16,80]{1,0:T(8,128)S(1)} %mul.16566), kind=kOutput, calls=%fused_computation.5 | convolution fusion | flops 1147594752 | bytes 33698816 | tf_op jit(solution)/shard_map/thd,khd->htk/dot_general | solution.py:102
  231.6 13.7 %exponential_reduce_fusion = f32[16,384]{1,0:T(8,128)S(1)} fusion(f32[16,384,1152]{2,1,0:T(8,128)} %get-tuple-element.459, f32[16,384]{1,0:T(8,128)S(1)} %get-tuple-element.458, pred[384,1152]{1,0:T(8,128)(4,1)S(1)} %copy-done.3), kind=kLoop, calls=%fused_computation.3 | loop fusion | flops 21227520 | bytes 28803072 | tf_op jit(solution)/shard_map/reduce_sum | solution.py:107
  245.3 13.1 %fusion.51 = bf16[16,80,384]{2,1,0:T(8,128)(2,1)} fusion(bf16[1152,16,80]{0,2,1:T(8,128)(2,1)S(1)} %bitcast.665, f32[16,384,1152]{2,1,0:T(8,128)} %get-tuple-element.459, f32[16,384]{1,0:T(8,128)S(1)} %log_add_fusion, pred[384,1152]{1,0:T(8,128)(4,1)S(1)} %copy-done.3), kind=kOutput, calls=%fused_computation.96 | convolution fusion | flops 1154187264 | bytes 32710656 | tf_op jit(solution)/shard_map/htk,khd->thd/dot_general | solution.py:110
  267.2 4.6 bitcast_dynamic-update-slice_fusion.3
  271.8 5.0 convert_reduce_fusion.1
  276.7 4.5 multiply_reduce_fusion.1
  289.8 24.5 %multiply_reduce_fusion = (f32[16,384]{1,0:T(8,128)S(1)}, f32[16,384,1152]{2,1,0:T(8,128)}) fusion(f32[16,384,1152]{2,1,0:T(8,128)} %get-tuple-element.459, f32[16,384]{1,0:T(8,128)S(1)} %log_add_fusion, pred[384,1152]{1,0:T(8,128)(4,1)} %fusion.50, bf16[384,16,80]{0,2,1:T(8,128)(2,1)} %bitcast.669, bf16[1152,16,80]{0,2,1:T(8,128)(2,1)} %bitcast.664), kind=kOutput, calls=%fused_computation.1 | convolution fusion | flops 1160767488 | bytes 61046784 | tf_op jit(solution)/shard_map/thd,khd->htk/dot_general | solution.py:139
  314.3 23.7 %multiply_convert_fusion = bf16[16,384,1152]{2,1,0:T(8,128)(2,1)} fusion(f32[16,384,1152]{2,1,0:T(8,128)} %get-tuple-element.464, f32[16,384,1152]{2,1,0:T(8,128)} %get-tuple-element.459, f32[16,384]{1,0:T(8,128)S(1)} %get-tuple-element.463, f32[16,384]{1,0:T(8,128)S(1)} %log_add_fusion, pred[384,1152]{1,0:T(8,128)(4,1)} %fusion.50), kind=kLoop, calls=%fused_computation | loop fusion | flops 35389440 | bytes 71270400 | tf_op jit(solution)/shard_map/convert_element_type | solution.py:141
  338.1 8.0 fusion.8
  354.1 14.2 %fusion.9 = bf16[1152,16,80]{0,2,1:T(8,128)(2,1)S(1)} fusion(bf16[384,16,80]{0,2,1:T(8,128)(2,1)} %bitcast.670, f32[16,384,1152]{2,1,0:T(8,128)} %get-tuple-element.459, f32[16,384]{1,0:T(8,128)S(1)} %log_add_fusion, pred[384,1152]{1,0:T(8,128)(4,1)} %fusion.50), kind=kOutput, calls=%fused_computation.23 | convolution fusion | flops 1155170304 | bytes 32710656 | tf_op jit(solution)/shard_map/htk,thd->khd/dot_general | solution.py:142
  380.8 11.7 fusion.44
  401.2 24.4 %reduce-scatter.11.cloned.1.call-done = bf16[256,1280]{1,0:T(8,128)(2,1)} async-done(((bf16[1024,1280]{1,0:T(8,128)(2,1)}), bf16[256,1280]{1,0:T(8,128)(2,1)}) %reduce-scatter.11.cloned.1.call-update) | async-done | bytes 655376 | tf_op jit(solution)/shard_map/reduce_scatter | solution.py:155
  431.0 9.2 fusion.43
  442.1 17.9 %convolution_convert_fusion = bf16[6,1280,1280]{2,1,0:T(8,128)(2,1)} fusion(bf16[6,384,1280]{2,1,0:T(8,128)(2,1)} %get-tuple-element.466, bf16[6,384,1280]{2,1,0:T(8,128)(2,1)} %bitcast_dynamic-update-slice_fusion), kind=kOutput, calls=%fused_computation.4 | convolution fusion | flops 7559577600 | bytes 31457280 | tf_op jit(solution)/shard_map/mto,mti->omi/dot_general | solution.py:172
  460.0 26.4 %copy.101 = bf16[1280,7680]{1,0:T(8,128)(2,1)} copy(bf16[1280,7680]{0,1:T(8,128)(2,1)} %bitcast.668) | data formatting | bytes 39321600
  489.6 6.5 fusion.27
  497.8 131.3 %reduce-scatter.13.cloned.1.call-done = bf16[320,7680]{1,0:T(8,128)(2,1)} async-done(((bf16[1280,7680]{1,0:T(8,128)(2,1)}), bf16[320,7680]{1,0:T(8,128)(2,1)}) %reduce-scatter.13.cloned.1.call-update) | async-done | bytes 4915216
  629.1 8.0 copy.102
  637.1 8.6 copy.91
  645.7 10.3 convert_add_fusion
  656.0 10.7 convolution_bitcast_fusion
  671.0 68.0 %all-reduce.5.cloned.1.call-done = (f32[320,8]{0,1:T(8,128)}, f32[320,8]{0,1:T(8,128)}, f32[320,8]{0,1:T(8,128)}, f32[320,8]{0,1:T(8,128)}, f32[320,8]{0,1:T(8,128)}, /*index=5*/f32[320,8]{0,1:T(8,128)}, f32[5,320]{1,0:T(8,128)}) async-done(((f32[320,8]{0,1:T(8,128)}, f32[320,8]{0,1:T(8,128)}, f32[320,8]{0,1:T(8,128)}, f32[320,8]{0,1:T(8,128)}, f32[320,8]{0,1:T(8,128)}, /*index=5*/f32[320,8]{0,1:T(8,128)}, ...) | async-done | bytes 67856 | tf_op jit(solution)/shard_map/psum | solution.py:198
  744.7 4.5 multiply_reduce_fusion.155
  758.7 5.1 multiply_reduce_fusion.153
  780.5 17.7 %subtract_multiply_fusion.35 = (f32[320,1,1]{0,2,1:T(1,128)S(1)}, f32[320,1,1]{0,2,1:T(1,128)S(1)}, f32[320,1,1]{0,2,1:T(1,128)S(1)}, f32[320,1,1]{0,2,1:T(1,128...) fusion(f32[320,1,1]{0,2,1:T(1,128)S(1)} %get-tuple-element.437, ...), kind=kLoop, calls=%fused_computation.622 | loop fusion | flops 20160 | bytes 19340 | tf_op jit(solution)/shard_map/mul | solution.py:32
  806.9 4.5 multiply_reduce_fusion.126
  820.9 5.1 multiply_reduce_fusion.124
  842.7 17.6 %subtract_multiply_fusion.28 = (f32[320,1,1]{0,2,1:T(1,128)S(1)}, f32[320,1,1]{0,2,1:T(1,128)S(1)}, f32[320,1,1]{0,2,1:T(1,128)S(1)}, f32[320,1,1]{0,2,1:T(1,128...) fusion(f32[320,1,1]{0,2,1:T(1,128)S(1)} %get-tuple-element.404, ...), kind=kLoop, calls=%fused_computation.566 | loop fusion | flops 20160 | bytes 19340 | tf_op jit(solution)/shard_map/mul | solution.py:32
  882.3 5.1 multiply_reduce_fusion.95
  904.0 17.6 %subtract_multiply_fusion.21 = (f32[320,1,1]{0,2,1:T(1,128)S(1)}, f32[320,1,1]{0,2,1:T(1,128)S(1)}, f32[320,1,1]{0,2,1:T(1,128)S(1)}, f32[320,1,1]{0,2,1:T(1,128...) fusion(f32[320,1,1]{0,2,1:T(1,128)S(1)} %get-tuple-element.371, ...), kind=kLoop, calls=%fused_computation.510 | loop fusion | flops 20160 | bytes 19340 | tf_op jit(solution)/shard_map/mul | solution.py:32
  943.7 5.1 multiply_reduce_fusion.66
  965.4 17.6 %subtract_multiply_fusion.14 = (f32[320,1,1]{0,2,1:T(1,128)S(1)}, f32[320,1,1]{0,2,1:T(1,128)S(1)}, f32[320,1,1]{0,2,1:T(1,128)S(1)}, f32[320,1,1]{0,2,1:T(1,128...) fusion(f32[320,1,1]{0,2,1:T(1,128)S(1)} %get-tuple-element.338, ...), kind=kLoop, calls=%fused_computation.454 | loop fusion | flops 20160 | bytes 19340 | tf_op jit(solution)/shard_map/mul | solution.py:32
  1005.1 5.1 multiply_reduce_fusion.37
  1026.8 17.6 %subtract_multiply_fusion.7 = (f32[320,1,1]{0,2,1:T(1,128)S(1)}, f32[320,1,1]{0,2,1:T(1,128)S(1)}, f32[320,1,1]{0,2,1:T(1,128)S(1)}, f32[320,1,1]{0,2,1:T(1,128)...) fusion(f32[320,1,1]{0,2,1:T(1,128)S(1)} %get-tuple-element.305, ...), kind=kLoop, calls=%fused_computation.398 | loop fusion | flops 20160 | bytes 19340 | tf_op jit(solution)/shard_map/mul | solution.py:32
  1052.7 4.5 multiply_reduce_fusion.10
  1058.0 4.5 multiply_reduce_fusion.9
  1066.7 4.9 multiply_reduce_fusion.8
  1088.3 17.5 %subtract_multiply_fusion = (f32[320,1,1]{0,2,1:T(1,128)S(1)}, f32[320,1,1]{0,2,1:T(1,128)S(1)}, f32[320,1,1]{0,2,1:T(1,128)S(1)}, f32[320,1,1]{0,2,1:T(1,128)S(...) fusion(f32[320,1,1]{0,2,1:T(1,128)S(1)} %get-tuple-element.272, f32[]{:T(128)S(6)} %rsqrt.263, ...), kind=kLoop, calls=%fused_computation.342 | loop fusion | flops 20160 | bytes 19340 | tf_op jit(solution)/shard_map/mul | solution.py:32
  1109.5 71.6 %all-reduce.7.cloned.1.call-done = (bf16[1,1280,8]{1,2,0:T(8,128)(2,1)}, bf16[1,1280,8]{1,2,0:T(8,128)(2,1)}, bf16[1,1280,8]{1,2,0:T(8,128)(2,1)}, bf16[1,1280,8...) async-done(((bf16[1,1280,8]{1,2,0:T(8,128)(2,1)}, bf16[1,1280,8]{1,2,0:T(8,128)(2,1)}, bf16[1,1280,8]{1,2,0:T(8,128)(2,1)}, ...) | async-done | bytes 122896 | tf_op jit(solution)/shard_map/psum | solution.py:203
  1185.5 12.8 %bitcast_subtract_fusion = (f32[320,6,1280]{2,0,1:T(8,128)}, f32[6,1280,320]{1,2,0:T(8,128)S(1)}) fusion(f32[320,6,1280]{2,0,1:T(8,128)} %convert_add_fusion, f32[6,1280,8]{1,2,0:T(8,128)S(1)} %convert_multiply_fusion.5, f32[320,6,8]{0,2,1:T(8,128)S(1)} %constant_dynamic-update-slice_fusion.8), kind=kOutput, calls=%fused_computation.7 | convolution fusion | flops 238387200 | bytes 29798400 | tf_op jit(solution)/shard_map/upt,pqt->upq/dot_general | solution.py:208
  (280 shorter events, 279.6 us)
Async XLA Ops:
  7.2 648.8 %copy-start = (f32[6,1280,8]{1,2,0:T(8,128)S(1)}, f32[6,1280,8]{1,2,0:T(8,128)}, u32[]{:S(2)}) copy-start(f32[6,1280,8]{1,2,0:T(8,128)} %param.14) | copy-start | bytes 737284
  7.2 7.8 copy-start.1
  7.2 129.4 %all-gather.7.cloned.1.call-start = ((), (), s32[]{:S(2)}) async-start(), calls=%async_computation.4 | async-start | bytes 24576000 | tf_op jit(solution)/shard_map/all_gather | solution.py:59
  7.9 167.5 %all-gather.9.cloned.1.call-start = ((), (), s32[]{:S(2)}) async-start(), calls=%async_computation.7 | async-start | bytes 3276800 | tf_op jit(solution)/shard_map/all_gather | solution.py:80
  14.3 132.7 %copy-start.25 = (f32[1280,5]{0,1:T(8,128)}, f32[1280,5]{0,1:T(8,128)S(1)}, u32[]{:S(2)}) copy-start(f32[1280,5]{0,1:T(8,128)S(1)} %reshape.8102) | copy-start | bytes 76804
  15.0 136.4 %copy-start.26 = (f32[1280]{0:T(1024)}, f32[1280]{0:T(1024)S(1)}, u32[]{:S(2)}) copy-start(f32[1280]{0:T(1024)S(1)} %get-tuple-element.55) | copy-start | bytes 15364
  15.0 138.7 %copy-start.22 = (f32[1280]{0:T(1024)}, f32[1280]{0:T(1024)S(1)}, u32[]{:S(2)}) copy-start(f32[1280]{0:T(1024)S(1)} %get-tuple-element.58) | copy-start | bytes 15364
  15.8 137.9 %copy-start.28 = (f32[384]{0:T(512)}, f32[384]{0:T(512)S(1)}, u32[]{:S(2)}) copy-start(f32[384]{0:T(512)S(1)} %get-tuple-element.453) | copy-start | bytes 4612
  149.7 53.4 %all-gather.11.cloned.1.call-start = ((), (), s32[]{:S(2)}) async-start(), calls=%async_computation.8 | async-start | bytes 3276800 | tf_op jit(solution)/shard_map/all_gather | solution.py:79
  150.5 248.2 %reduce-scatter.9.cloned.1.call-start = ((), (), s32[]{:S(2)}) async-start(), calls=%async_computation.5 | async-start | bytes 3276800 | tf_op jit(solution)/shard_map/reduce_scatter | solution.py:152
  154.0 2.4 copy-start.24
  218.6 13.1 %copy-start.3 = (pred[384,1152]{1,0:T(8,128)(4,1)S(1)}, pred[384,1152]{1,0:T(8,128)(4,1)}, u32[]{:S(2)}) copy-start(pred[384,1152]{1,0:T(8,128)(4,1)} %fusion.50) | copy-start | bytes 1327108
  231.6 13.7 %copy-start.2 = (bf16[1152,1280]{0,1:T(8,128)(2,1)S(1)}, bf16[1152,1280]{0,1:T(8,128)(2,1)}, u32[]{:S(2)}) copy-start(bf16[1152,1280]{0,1:T(8,128)(2,1)} %copy.80) | copy-start | bytes 8847364
  260.9 4.0 copy-start.12
  264.9 16.4 %copy-start.9 = (f32[384,1280]{1,0:T(8,128)}, f32[384,1280]{1,0:T(8,128)S(1)}, u32[]{:S(2)}) copy-start(f32[384,1280]{1,0:T(8,128)S(1)} %get-tuple-element.461) | copy-start | bytes 5898244
  267.2 4.6 copy-start.10
  271.7 5.0 copy-start.42
  276.7 4.5 copy-start.17
  354.0 71.6 %reduce-scatter.11.cloned.1.call-start = ((), (), s32[]{:S(2)}) async-start(), calls=%async_computation.6 | async-start | bytes 3276800 | tf_op jit(solution)/shard_map/reduce_scatter | solution.py:155
  376.2 3.7 slice-start
  376.2 119.9 %reduce-scatter.15.cloned.1.call-start = ((), (), s32[]{:S(2)}) async-start(), calls=%async_computation.10 | async-start | bytes 819200
  392.5 2.1 copy-start.39
  392.5 2.1 copy-start.38
  392.5 4.8 copy-start.27
  397.3 28.3 %copy-start.14 = (bf16[1,128,1280]{2,1,0:T(8,128)(2,1)S(1)}, bf16[1,128,1280]{2,1,0:T(8,128)(2,1)}, u32[]{:S(2)}) copy-start(bf16[1,128,1280]{2,1,0:T(8,128)(2,1)} %copy.88) | copy-start | bytes 983044
  398.7 29.2 %copy-start.6 = (f32[384,1280]{1,0:T(8,128)S(1)}, f32[384,1280]{1,0:T(8,128)}, u32[]{:S(2)}) copy-start(f32[384,1280]{1,0:T(8,128)} %copy-done.5) | copy-start | bytes 5898244
  425.6 3.3 copy-start.18
  425.6 4.3 copy-start.11
  427.9 3.1 copy-start.15
  427.9 3.1 copy-start.19
  427.9 3.1 copy-start.20
  427.9 3.1 copy-start.21
  427.9 3.1 copy-start.23
  427.9 3.1 copy-start.29
  431.0 9.2 copy-start.30
  442.1 187.0 %reduce-scatter.13.cloned.1.call-start = ((), (), s32[]{:S(2)}) async-start(), calls=%async_computation.9 | async-start | bytes 24576000
  486.4 3.2 copy-start.40
  486.4 252.5 %all-reduce.5.cloned.1.call-start = ((), (), s32[]{:S(2)}) async-start(), calls=%async_computation.11 | async-start | bytes 172032 | tf_op jit(solution)/shard_map/psum | solution.py:198
  656.0 11.7 copy-start.37
  667.3 513.8 %all-reduce.7.cloned.1.call-start = ((), (), s32[]{:S(2)}) async-start(), calls=%async_computation.12 | async-start | bytes 245760 | tf_op jit(solution)/shard_map/psum | solution.py:203
  739.0 124.4 %copy-start.34 = (f32[320,8]{0,1:T(8,128)S(1)}, f32[320,8]{0,1:T(8,128)}, u32[]{:S(2)}) copy-start(f32[320,8]{0,1:T(8,128)} %get-tuple-element.223) | copy-start | bytes 30724
  798.1 126.5 %copy-start.33 = (f32[320,8]{0,1:T(8,128)S(1)}, f32[320,8]{0,1:T(8,128)}, u32[]{:S(2)}) copy-start(f32[320,8]{0,1:T(8,128)} %get-tuple-element.224) | copy-start | bytes 30724
  860.3 125.8 %copy-start.32 = (f32[320,8]{0,1:T(8,128)S(1)}, f32[320,8]{0,1:T(8,128)}, u32[]{:S(2)}) copy-start(f32[320,8]{0,1:T(8,128)} %get-tuple-element.225) | copy-start | bytes 30724
  921.6 125.8 %copy-start.31 = (f32[320,8]{0,1:T(8,128)S(1)}, f32[320,8]{0,1:T(8,128)}, u32[]{:S(2)}) copy-start(f32[320,8]{0,1:T(8,128)} %get-tuple-element.226) | copy-start | bytes 30724
  983.0 125.8 %copy-start.35 = (f32[5,320]{1,0:T(8,128)S(1)}, f32[5,320]{1,0:T(8,128)}, u32[]{:S(2)}) copy-start(f32[5,320]{1,0:T(8,128)} %param.16) | copy-start | bytes 19204
  983.1 125.8 %copy-start.36 = (f32[5,320]{1,0:T(8,128)S(1)}, f32[5,320]{1,0:T(8,128)}, u32[]{:S(2)}) copy-start(f32[5,320]{1,0:T(8,128)} %get-tuple-element.227) | copy-start | bytes 19204
  1185.5 12.9 %copy-start.16 = (f32[6,1280,8]{1,2,0:T(8,128)}, f32[6,1280,8]{1,2,0:T(8,128)S(1)}, u32[]{:S(2)}) copy-start(f32[6,1280,8]{1,2,0:T(8,128)S(1)} %convert_multiply_fusion.5) | copy-start | bytes 737284
  1185.5 12.8 %copy-start.8 = (f32[320,6,160]{2,0,1:T(8,128)S(1)}, f32[320,6,160]{2,0,1:T(8,128)}, u32[]{:S(2)}) copy-start(f32[320,6,160]{2,0,1:T(8,128)} %copy.92) | copy-start | bytes 3686404
  (5 other events, 6.9 us)
Sparse Core Ops, SparseCore 0:
  9.6 126.9 all-gather.6
  149.9 25.5 all-gather.8
  177.6 25.5 all-gather.10
  354.1 34.4 reduce-scatter.8
  391.1 34.5 reduce-scatter.10
  442.2 22.4 reduce-scatter.14
  486.6 142.4 reduce-scatter.12
  667.5 71.4 all-reduce.4
  1109.6 71.4 all-reduce.6
where the time goes:
time: 1230 us; the launch traced here: 1220 us
  waiting for transfers between devices  457 us (37%)
  other arithmetic  393 us (32%)
  matrix products  192 us (16%)
  local copies, waits for them, and re-layouts  118 us (10%)
  between operations  47.3 us (4%)
    reduce_sum x60, other arithmetic, orthonormal(): jnp.sum(earlier * column, axis=-2, keepdims=True) * earlier  164 us
    unnamed x11, waiting for transfers between devices  133 us
    all_gather x1, waiting for transfers between devices, on_device(): lax.all_gather(weights, 'zero', axis=0, tiled=True)  121 us
    mul x6, other arithmetic, orthonormal(): column * lax.rsqrt(jnp.sum(column * column, axis=-2, keepdims=True) + EPS)  106 us
    psum x1, waiting for transfers between devices, on_device(): lax.psum(right_term.astype(jnp.bfloat16), 'rep').astype(jnp.float32)  71.6 us
    psum x1, waiting for transfers between devices, on_device(): left_sum = lax.psum(local_left_factor[:, mat_index], 'rep')  68 us
    unnamed x106, local copies, waits for them, and re-layouts  62 us
    reduce_sum x30, other arithmetic, orthonormal(): jnp.sum(column * column, axis=-2, keepdims=True) + EPS  49.2 us
  transfers between devices with their start and end apart: 9, of which 7 were waited for; matrix products, arithmetic and copies ran while one was open for 9% of the time, Pallas kernels for 0%

commit v1 on v0

--- a/solution.py
+++ b/solution.py
@@ -11,6 +11,10 @@
 LOG2E = 1.442695041
 NEG = -1e30
 PRECISION_HIGH = lax.Precision.HIGHEST
+
+
+def deliver_trails(local_block):
+    return lax.all_gather(local_block, "rep").sum(axis=0)
 
 
 def rms_scale(field):
@@ -200,7 +204,7 @@
         right_term = jnp.einsum(
             "oi,or->ir", combined_result[:, mat_index], left_ortho, precision=PRECISION_HIGH
         )
-        right_parts.append(lax.psum(right_term.astype(jnp.bfloat16), "rep").astype(jnp.float32))
+        right_parts.append(deliver_trails(right_term.astype(jnp.bfloat16)).astype(jnp.float32))
         left_parts.append(left_ortho)
     orthogonalized = jnp.stack(left_parts, axis=1)
     right_total = jnp.stack(right_parts, axis=0)

time: 1230 us -> 1330 us (1.081)
  blocking collectives: 6.25 us -> 190 us
  waiting for transfers between devices: 457 us -> 386 us
    all_gather x0 -> x6, blocking collectives: none -> 184 us  [deliver_trails(): return lax.all_gather(local_block, 'rep').sum(axis=0)]
    psum x1 -> x0, waiting for transfers between devices: 71.6 us -> none  [on_device(): lax.psum(right_term.astype(jnp.bfloat16), 'rep').astype(jnp.float32)]
    unnamed x11 -> x10, waiting for transfers between devices: 133 us -> 133 us
  transfers between devices with their start and end apart: 9 -> 8, of which waited for: 7 -> 6; matrix products, arithmetic and copies ran while one was open for 9% -> 9% of each run, Pallas kernels for 0% -> 0%
where the time goes in v1:
time: 1330 us; the launch traced here: 1320 us
  other arithmetic  392 us (29%)
  waiting for transfers between devices  386 us (29%)
  blocking collectives  190 us (14%)
  matrix products  188 us (14%)
  local copies, waits for them, and re-layouts  114 us (9%)
  between operations  48.3 us (4%)
    all_gather x6, blocking collectives, deliver_trails(): return lax.all_gather(local_block, 'rep').sum(axis=0)  184 us
    reduce_sum x60, other arithmetic, orthonormal(): jnp.sum(earlier * column, axis=-2, keepdims=True) * earlier  163 us
    unnamed x10, waiting for transfers between devices  133 us
    all_gather x1, waiting for transfers between devices, on_device(): lax.all_gather(weights, 'zero', axis=0, tiled=True)  121 us
    mul x6, other arithmetic, orthonormal(): column * lax.rsqrt(jnp.sum(column * column, axis=-2, keepdims=True) + EPS)  106 us
    psum x1, waiting for transfers between devices, on_device(): left_sum = lax.psum(local_left_factor[:, mat_index], 'rep')  68.3 us
    unnamed x106, local copies, waits for them, and re-layouts  58.4 us
    reduce_sum x30, other arithmetic, orthonormal(): jnp.sum(column * column, axis=-2, keepdims=True) + EPS  48.9 us
  transfers between devices with their start and end apart: 8, of which 6 were waited for; matrix products, arithmetic and copies ran while one was open for 9% of the time, Pallas kernels for 0%

profile of v1, /device:TPU:0, one launch (start us, length us, event | category | flops | bytes accessed | tf_op | source)
XLA Modules:
  0.0 1319.5 jit_solution(16348582098666399118)
XLA Ops:
  8.0 6.2 all-gather.8
  15.9 120.7 %all-gather.13.cloned.1.call-done = bf16[1280,6,1280]{2,0,1:T(8,128)(2,1)} async-done(((bf16[320,6,1280]{2,0,1:T(8,128)(2,1)}), bf16[1280,6,1280]{2,0,1:T(8,128)(2,1)}) %all-gather.13.cloned.1.call-update) | async-done | bytes 19660816 | tf_op jit(solution)/shard_map/all_gather | solution.py:63
  136.6 10.4 fusion.109
  163.3 12.1 all-gather.15.cloned.1.call-done
  175.4 27.7 %all-gather.17.cloned.1.call-done = bf16[1,1024,1280]{2,1,0:T(8,128)(2,1)} async-done(((bf16[1,256,1280]{2,1,0:T(8,128)(2,1)}), bf16[1,1024,1280]{2,1,0:T(8,128)(2,1)}) %all-gather.17.cloned.1.call-update) | async-done | bytes 2621456 | tf_op jit(solution)/shard_map/all_gather | solution.py:83
  203.1 4.6 pad_maximum_fusion
  207.7 5.4 copy.80
  213.2 5.4 copy.82
  218.6 13.1 select_reduce_fusion
  231.6 13.7 %exponential_reduce_fusion = f32[16,384]{1,0:T(8,128)S(1)} fusion(f32[16,384,1152]{2,1,0:T(8,128)} %get-tuple-element.453, f32[16,384]{1,0:T(8,128)S(1)} %get-tuple-element.452, pred[384,1152]{1,0:T(8,128)(4,1)S(1)} %copy-done.3), kind=kLoop, calls=%fused_computation.3 | loop fusion | flops 21227520 | bytes 28803072 | tf_op jit(solution)/shard_map/reduce_sum | solution.py:111
  245.3 13.1 fusion.45
  271.8 5.0 convert_reduce_fusion.1
  289.8 24.5 %multiply_reduce_fusion = (f32[16,384]{1,0:T(8,128)S(1)}, f32[16,384,1152]{2,1,0:T(8,128)}) fusion(f32[16,384,1152]{2,1,0:T(8,128)} %get-tuple-element.453, f32[16,384]{1,0:T(8,128)S(1)} %log_add_fusion, pred[384,1152]{1,0:T(8,128)(4,1)} %fusion.44, bf16[384,16,80]{0,2,1:T(8,128)(2,1)} %bitcast.675, bf16[1152,16,80]{0,2,1:T(8,128)(2,1)} %bitcast.670), kind=kOutput, calls=%fused_computation.1 | convolution fusion | flops 1160767488 | bytes 61046784 | tf_op jit(solution)/shard_map/thd,khd->htk/dot_general | solution.py:143
  314.3 23.7 %multiply_convert_fusion = bf16[16,384,1152]{2,1,0:T(8,128)(2,1)} fusion(f32[16,384,1152]{2,1,0:T(8,128)} %get-tuple-element.458, f32[16,384,1152]{2,1,0:T(8,128)} %get-tuple-element.453, f32[16,384]{1,0:T(8,128)S(1)} %get-tuple-element.457, f32[16,384]{1,0:T(8,128)S(1)} %log_add_fusion, pred[384,1152]{1,0:T(8,128)(4,1)} %fusion.44), kind=kLoop, calls=%fused_computation | loop fusion | flops 35389440 | bytes 71270400 | tf_op jit(solution)/shard_map/convert_element_type | solution.py:145
  338.1 8.0 fusion.8
  354.1 14.2 %fusion.9 = bf16[1152,16,80]{0,2,1:T(8,128)(2,1)S(1)} fusion(bf16[384,16,80]{0,2,1:T(8,128)(2,1)} %bitcast.676, f32[16,384,1152]{2,1,0:T(8,128)} %get-tuple-element.453, f32[16,384]{1,0:T(8,128)S(1)} %log_add_fusion, pred[384,1152]{1,0:T(8,128)(4,1)} %fusion.44), kind=kOutput, calls=%fused_computation.23 | convolution fusion | flops 1155170304 | bytes 32710656 | tf_op jit(solution)/shard_map/htk,thd->khd/dot_general | solution.py:146
  380.8 11.7 fusion.38
  401.2 24.4 %reduce-scatter.11.cloned.1.call-done = bf16[256,1280]{1,0:T(8,128)(2,1)} async-done(((bf16[1024,1280]{1,0:T(8,128)(2,1)}), bf16[256,1280]{1,0:T(8,128)(2,1)}) %reduce-scatter.11.cloned.1.call-update) | async-done | bytes 655376 | tf_op jit(solution)/shard_map/reduce_scatter | solution.py:159
  431.0 9.2 fusion.37
  442.1 17.9 %convolution_convert_fusion = bf16[6,1280,1280]{2,1,0:T(8,128)(2,1)} fusion(bf16[6,384,1280]{2,1,0:T(8,128)(2,1)} %get-tuple-element.460, bf16[6,384,1280]{2,1,0:T(8,128)(2,1)} %bitcast_dynamic-update-slice_fusion), kind=kOutput, calls=%fused_computation.4 | convolution fusion | flops 7559577600 | bytes 31457280 | tf_op jit(solution)/shard_map/mto,mti->omi/dot_general | solution.py:176
  460.0 26.4 %copy.101 = bf16[1280,7680]{1,0:T(8,128)(2,1)} copy(bf16[1280,7680]{0,1:T(8,128)(2,1)} %bitcast.674) | data formatting | bytes 39321600
  489.6 6.5 fusion.27
  497.8 131.3 %reduce-scatter.13.cloned.1.call-done = bf16[320,7680]{1,0:T(8,128)(2,1)} async-done(((bf16[1280,7680]{1,0:T(8,128)(2,1)}), bf16[320,7680]{1,0:T(8,128)(2,1)}) %reduce-scatter.13.cloned.1.call-update) | async-done | bytes 4915216
  629.1 8.0 copy.102
  637.1 8.6 copy.91
  645.7 10.3 convert_add_fusion
  656.0 10.7 convolution_bitcast_fusion
  670.7 68.3 %all-reduce.3.cloned.1.call-done = (f32[320,8]{0,1:T(8,128)}, f32[320,8]{0,1:T(8,128)}, f32[320,8]{0,1:T(8,128)}, f32[320,8]{0,1:T(8,128)}, f32[320,8]{0,1:T(8,128)}, /*index=5*/f32[320,8]{0,1:T(8,128)}, f32[5,320]{1,0:T(8,128)}) async-done(((f32[320,8]{0,1:T(8,128)}, f32[320,8]{0,1:T(8,128)}, f32[320,8]{0,1:T(8,128)}, f32[320,8]{0,1:T(8,128)}, f32[320,8]{0,1:T(8,128)}, /*index=5*/f32[320,8]{0,1:T(8,128)}, ...) | async-done | bytes 67856 | tf_op jit(solution)/shard_map/psum | solution.py:202
  758.9 5.0 multiply_reduce_fusion.153
  780.6 17.6 %subtract_multiply_fusion.35 = (f32[320,1,1]{0,2,1:T(1,128)S(1)}, f32[320,1,1]{0,2,1:T(1,128)S(1)}, f32[320,1,1]{0,2,1:T(1,128)S(1)}, f32[320,1,1]{0,2,1:T(1,128...) fusion(f32[320,1,1]{0,2,1:T(1,128)S(1)} %get-tuple-element.431, ...), kind=kLoop, calls=%fused_computation.616 | loop fusion | flops 20160 | bytes 19340 | tf_op jit(solution)/shard_map/mul | solution.py:36
  800.7 30.6 %all-gather.2 = bf16[10240,8]{0,1:T(8,128)(2,1)S(1)} all-gather(bf16[1280,8]{0,1:T(8,128)(2,1)S(1)} %convolution_convert_fusion.8), channel_id=4, replica_groups=mesh['rep'=8,'zero'=4] {'rep'}, dimensions={0}, use_global_device_ids=true | all-gather | bytes 184320 | tf_op jit(solution)/shard_map/all_gather | solution.py:17
  851.1 5.1 multiply_reduce_fusion.124
  872.7 17.6 %subtract_multiply_fusion.28 = (f32[320,1,1]{0,2,1:T(1,128)S(1)}, f32[320,1,1]{0,2,1:T(1,128)S(1)}, f32[320,1,1]{0,2,1:T(1,128)S(1)}, f32[320,1,1]{0,2,1:T(1,128...) fusion(f32[320,1,1]{0,2,1:T(1,128)S(1)} %get-tuple-element.398, ...), kind=kLoop, calls=%fused_computation.560 | loop fusion | flops 20160 | bytes 19340 | tf_op jit(solution)/shard_map/mul | solution.py:36
  892.7 30.8 %all-gather.3 = bf16[10240,8]{0,1:T(8,128)(2,1)S(1)} all-gather(bf16[1280,8]{0,1:T(8,128)(2,1)S(1)} %convolution_convert_fusion.7), channel_id=5, replica_groups=mesh['rep'=8,'zero'=4] {'rep'}, dimensions={0}, use_global_device_ids=true | all-gather | bytes 184320 | tf_op jit(solution)/shard_map/all_gather | solution.py:17
  942.8 4.9 multiply_reduce_fusion.95
  964.0 17.6 %subtract_multiply_fusion.21 = (f32[320,1,1]{0,2,1:T(1,128)S(1)}, f32[320,1,1]{0,2,1:T(1,128)S(1)}, f32[320,1,1]{0,2,1:T(1,128)S(1)}, f32[320,1,1]{0,2,1:T(1,128...) fusion(f32[320,1,1]{0,2,1:T(1,128)S(1)} %get-tuple-element.365, ...), kind=kLoop, calls=%fused_computation.504 | loop fusion | flops 20160 | bytes 19340 | tf_op jit(solution)/shard_map/mul | solution.py:36
  984.0 30.6 %all-gather.4 = bf16[10240,8]{0,1:T(8,128)(2,1)S(1)} all-gather(bf16[1280,8]{0,1:T(8,128)(2,1)S(1)} %convolution_convert_fusion.6), channel_id=6, replica_groups=mesh['rep'=8,'zero'=4] {'rep'}, dimensions={0}, use_global_device_ids=true | all-gather | bytes 184320 | tf_op jit(solution)/shard_map/all_gather | solution.py:17
  1033.8 5.0 multiply_reduce_fusion.66
  1055.5 17.6 %subtract_multiply_fusion.14 = (f32[320,1,1]{0,2,1:T(1,128)S(1)}, f32[320,1,1]{0,2,1:T(1,128)S(1)}, f32[320,1,1]{0,2,1:T(1,128)S(1)}, f32[320,1,1]{0,2,1:T(1,128...) fusion(f32[320,1,1]{0,2,1:T(1,128)S(1)} %get-tuple-element.332, ...), kind=kLoop, calls=%fused_computation.448 | loop fusion | flops 20160 | bytes 19340 | tf_op jit(solution)/shard_map/mul | solution.py:36
  1075.5 30.6 %all-gather.5 = bf16[10240,8]{0,1:T(8,128)(2,1)S(1)} all-gather(bf16[1280,8]{0,1:T(8,128)(2,1)S(1)} %convolution_convert_fusion.5), channel_id=7, replica_groups=mesh['rep'=8,'zero'=4] {'rep'}, dimensions={0}, use_global_device_ids=true | all-gather | bytes 184320 | tf_op jit(solution)/shard_map/all_gather | solution.py:17
  1125.1 5.1 multiply_reduce_fusion.37
  1146.9 17.5 %subtract_multiply_fusion.7 = (f32[320,1,1]{0,2,1:T(1,128)S(1)}, f32[320,1,1]{0,2,1:T(1,128)S(1)}, f32[320,1,1]{0,2,1:T(1,128)S(1)}, f32[320,1,1]{0,2,1:T(1,128)...) fusion(f32[320,1,1]{0,2,1:T(1,128)S(1)} %get-tuple-element.299, ...), kind=kLoop, calls=%fused_computation.392 | loop fusion | flops 20160 | bytes 19340 | tf_op jit(solution)/shard_map/mul | solution.py:36
  1166.8 30.6 %all-gather.6 = bf16[10240,8]{0,1:T(8,128)(2,1)S(1)} all-gather(bf16[1280,8]{0,1:T(8,128)(2,1)S(1)} %convolution_convert_fusion.4), channel_id=8, replica_groups=mesh['rep'=8,'zero'=4] {'rep'}, dimensions={0}, use_global_device_ids=true | all-gather | bytes 184320 | tf_op jit(solution)/shard_map/all_gather | solution.py:17
  1202.8 4.6 multiply_reduce_fusion.10
  1216.9 4.9 multiply_reduce_fusion.8
  1238.0 17.7 %subtract_multiply_fusion = (f32[320,1,1]{0,2,1:T(1,128)S(1)}, f32[320,1,1]{0,2,1:T(1,128)S(1)}, f32[320,1,1]{0,2,1:T(1,128)S(1)}, f32[320,1,1]{0,2,1:T(1,128)S(...) fusion(f32[320,1,1]{0,2,1:T(1,128)S(1)} %get-tuple-element.266, f32[]{:T(128)S(6)} %rsqrt.263, ...), kind=kLoop, calls=%fused_computation.336 | loop fusion | flops 20160 | bytes 19340 | tf_op jit(solution)/shard_map/mul | solution.py:36
  1258.1 30.9 %all-gather.7 = bf16[10240,8]{0,1:T(8,128)(2,1)S(1)} all-gather(bf16[1280,8]{0,1:T(8,128)(2,1)S(1)} %convolution_convert_fusion.3), channel_id=9, replica_groups=mesh['rep'=8,'zero'=4] {'rep'}, dimensions={0}, use_global_device_ids=true | all-gather | bytes 184320 | tf_op jit(solution)/shard_map/all_gather | solution.py:17
  1289.2 12.4 bitcast_subtract_fusion
  (289 shorter events, 293.2 us)
Async XLA Ops:
  7.2 648.8 %copy-start = (f32[6,1280,8]{1,2,0:T(8,128)S(1)}, f32[6,1280,8]{1,2,0:T(8,128)}, u32[]{:S(2)}) copy-start(f32[6,1280,8]{1,2,0:T(8,128)} %param.14) | copy-start | bytes 737284
  7.2 7.8 copy-start.1
  7.2 129.4 %all-gather.13.cloned.1.call-start = ((), (), s32[]{:S(2)}) async-start(), calls=%async_computation.4 | async-start | bytes 24576000 | tf_op jit(solution)/shard_map/all_gather | solution.py:63
  7.9 167.5 %all-gather.15.cloned.1.call-start = ((), (), s32[]{:S(2)}) async-start(), calls=%async_computation.7 | async-start | bytes 3276800 | tf_op jit(solution)/shard_map/all_gather | solution.py:84
  14.3 132.7 %copy-start.25 = (f32[1280,5]{0,1:T(8,128)}, f32[1280,5]{0,1:T(8,128)S(1)}, u32[]{:S(2)}) copy-start(f32[1280,5]{0,1:T(8,128)S(1)} %reshape.8162) | copy-start | bytes 76804
  15.0 136.4 %copy-start.26 = (f32[1280]{0:T(1024)}, f32[1280]{0:T(1024)S(1)}, u32[]{:S(2)}) copy-start(f32[1280]{0:T(1024)S(1)} %get-tuple-element.55) | copy-start | bytes 15364
  15.0 138.7 %copy-start.22 = (f32[1280]{0:T(1024)}, f32[1280]{0:T(1024)S(1)}, u32[]{:S(2)}) copy-start(f32[1280]{0:T(1024)S(1)} %get-tuple-element.58) | copy-start | bytes 15364
  15.8 137.9 %copy-start.28 = (f32[384]{0:T(512)}, f32[384]{0:T(512)S(1)}, u32[]{:S(2)}) copy-start(f32[384]{0:T(512)S(1)} %get-tuple-element.447) | copy-start | bytes 4612
  149.7 53.4 %all-gather.17.cloned.1.call-start = ((), (), s32[]{:S(2)}) async-start(), calls=%async_computation.8 | async-start | bytes 3276800 | tf_op jit(solution)/shard_map/all_gather | solution.py:83
  150.5 248.2 %reduce-scatter.9.cloned.1.call-start = ((), (), s32[]{:S(2)}) async-start(), calls=%async_computation.5 | async-start | bytes 3276800 | tf_op jit(solution)/shard_map/reduce_scatter | solution.py:156
  154.0 2.4 copy-start.24
  218.6 13.1 copy-start.3
  231.6 13.7 %copy-start.2 = (bf16[1152,1280]{0,1:T(8,128)(2,1)S(1)}, bf16[1152,1280]{0,1:T(8,128)(2,1)}, u32[]{:S(2)}) copy-start(bf16[1152,1280]{0,1:T(8,128)(2,1)} %copy.80) | copy-start | bytes 8847364
  260.9 4.0 copy-start.12
  264.9 16.4 %copy-start.9 = (f32[384,1280]{1,0:T(8,128)}, f32[384,1280]{1,0:T(8,128)S(1)}, u32[]{:S(2)}) copy-start(f32[384,1280]{1,0:T(8,128)S(1)} %get-tuple-element.455) | copy-start | bytes 5898244
  267.2 4.6 copy-start.10
  271.7 5.0 copy-start.42
  276.7 4.5 copy-start.17
  346.1 1.7 copy-start.4
  354.0 71.6 %reduce-scatter.11.cloned.1.call-start = ((), (), s32[]{:S(2)}) async-start(), calls=%async_computation.6 | async-start | bytes 3276800 | tf_op jit(solution)/shard_map/reduce_scatter | solution.py:159
  376.2 3.7 slice-start
  376.2 119.9 %reduce-scatter.15.cloned.1.call-start = ((), (), s32[]{:S(2)}) async-start(), calls=%async_computation.10 | async-start | bytes 819200
  392.5 2.1 copy-start.39
  392.5 2.1 copy-start.38
  392.5 4.8 copy-start.27
  397.3 28.3 %copy-start.14 = (bf16[1,128,1280]{2,1,0:T(8,128)(2,1)S(1)}, bf16[1,128,1280]{2,1,0:T(8,128)(2,1)}, u32[]{:S(2)}) copy-start(bf16[1,128,1280]{2,1,0:T(8,128)(2,1)} %copy.88) | copy-start | bytes 983044
  398.7 29.2 %copy-start.6 = (f32[384,1280]{1,0:T(8,128)S(1)}, f32[384,1280]{1,0:T(8,128)}, u32[]{:S(2)}) copy-start(f32[384,1280]{1,0:T(8,128)} %copy-done.5) | copy-start | bytes 5898244
  425.6 3.3 copy-start.18
  425.6 4.3 copy-start.11
  427.9 3.1 copy-start.15
  427.9 3.1 copy-start.19
  427.9 3.1 copy-start.20
  427.9 3.1 copy-start.21
  427.9 3.1 copy-start.23
  427.9 3.1 copy-start.29
  431.0 9.2 copy-start.30
  442.1 187.0 %reduce-scatter.13.cloned.1.call-start = ((), (), s32[]{:S(2)}) async-start(), calls=%async_computation.9 | async-start | bytes 24576000
  486.4 3.2 copy-start.40
  486.4 252.5 %all-reduce.3.cloned.1.call-start = ((), (), s32[]{:S(2)}) async-start(), calls=%async_computation.11 | async-start | bytes 172032 | tf_op jit(solution)/shard_map/psum | solution.py:202
  656.0 11.4 copy-start.37
  739.0 184.6 %copy-start.34 = (f32[320,8]{0,1:T(8,128)S(1)}, f32[320,8]{0,1:T(8,128)}, u32[]{:S(2)}) copy-start(f32[320,8]{0,1:T(8,128)} %get-tuple-element.223) | copy-start | bytes 30724
  800.7 213.9 %copy-start.33 = (f32[320,8]{0,1:T(8,128)S(1)}, f32[320,8]{0,1:T(8,128)}, u32[]{:S(2)}) copy-start(f32[320,8]{0,1:T(8,128)} %get-tuple-element.224) | copy-start | bytes 30724
  892.7 213.4 %copy-start.32 = (f32[320,8]{0,1:T(8,128)S(1)}, f32[320,8]{0,1:T(8,128)}, u32[]{:S(2)}) copy-start(f32[320,8]{0,1:T(8,128)} %get-tuple-element.225) | copy-start | bytes 30724
  984.0 213.5 %copy-start.31 = (f32[320,8]{0,1:T(8,128)S(1)}, f32[320,8]{0,1:T(8,128)}, u32[]{:S(2)}) copy-start(f32[320,8]{0,1:T(8,128)} %get-tuple-element.226) | copy-start | bytes 30724
  1289.1 12.5 copy-start.16
  1289.2 12.5 copy-start.8
  1307.0 4.5 copy-start.35
  1307.0 4.5 copy-start.36
  (4 other events, 5.2 us)
Sparse Core Ops, SparseCore 0:
  9.6 126.9 all-gather.12
  149.9 25.5 all-gather.14
  177.6 25.5 all-gather.16
  354.1 34.4 reduce-scatter.8
  391.1 34.5 reduce-scatter.10
  442.2 22.4 reduce-scatter.14
  486.6 142.4 reduce-scatter.12
  667.5 71.4 all-reduce.2
